TPU v7x, 256 devices: a whole 4x4x8 slice. The times are simulated.
256 devices in a mesh: row: 16 (over z, core), col: 16 (over y, x).
Axes of the slice: x: 4, y: 4, z: 8, core: 2. Of those that a mesh axis runs over, the one named last changes fastest.
Arguments:
- start_block: float32 [4096, 64, 128], P(('row', 'col')), may hold values from -2700 to 2700
- tile_values: bfloat16 [65536, 128, 128], P(('row', 'col')), may hold values from -3.535534 to 3.535534
- tile_rows: int32 [65536], P(('row', 'col')), may hold values from 0 to 15
- tile_cols: int32 [65536], P(('row', 'col')), may hold values from 0 to 79
- tile_count: int32 [256], P(('row', 'col')), may hold values from 32 to 256, as said below
- send_rows: int32 [256, 256, 32], P(('row', 'col')), may hold values from 0 to 2047
- send_count: int32 [256, 256], P(('row', 'col')), may hold values from 16 to 32, as said below
- rotation: float32 [192, 64], replicated, may hold values from -0.4375 to 0.4375
Outputs:
- embedding: float32 [4096, 64, 128], P(('row', 'col'))
Inputs may be any that keep to these rules, and one draw needn't show every extreme that they name: `tile_cols`: source tiles below 16 are the partition's own row tiles, the others its halo tiles. `tile_count`: slots at or past the count are ignored; some partition fills all 256 slots. `send_count`: slots at or past the count carry zeros; every partition fills all 32 slots for some peer, and some partition receives 32 rows from every partition.
All inputs are finite; a program needn't handle non-finite values.
Results may differ from a plain program's by a relative error of at most 0.0029.
Values may be sent and summed in bfloat16 or wider, within the bound.
A program may use at most 64 MiB of HBM per device.

v0:
```python
import jax
import jax.numpy as jnp
from jax import lax
from jax.sharding import PartitionSpec as P

HIGHEST_PRECISION = lax.Precision.HIGHEST


def local_inner(left_block, right_block):
    return jnp.einsum("tai,tbi->ab", left_block, right_block, precision=HIGHEST_PRECISION)


def unit_columns(product_block, gram_matrix):
    factor = jnp.linalg.cholesky(gram_matrix)
    inverse = lax.linalg.triangular_solve(
        factor, jnp.eye(factor.shape[0], dtype=jnp.float32), left_side=True, lower=True
    )
    return jnp.einsum("ab,tbi->tai", inverse, product_block, precision=HIGHEST_PRECISION)


def apply_graph(current, tile_values, tile_rows, tile_cols, tile_count, send_rows, send_count):
    row_tiles, block_width, tile_size = current.shape
    rounded = current.astype(jnp.bfloat16)
    node_rows = rounded.transpose(0, 2, 1).reshape(row_tiles * tile_size, block_width)
    targets = send_rows[0]
    partitions, capacity = targets.shape
    chosen = node_rows[targets.reshape(-1)].reshape(partitions, capacity, block_width)
    kept_slots = jnp.arange(capacity, dtype=jnp.int32)[None, :] < send_count[0][:, None]
    chosen = jnp.where(kept_slots[:, :, None], chosen, jnp.zeros_like(chosen))
    outgoing = chosen.reshape(lax.axis_size("row"), lax.axis_size("col"), capacity * block_width)
    incoming = lax.all_to_all(
        lax.all_to_all(outgoing, "row", split_axis=0, concat_axis=0, tiled=True),
        "col",
        split_axis=1,
        concat_axis=1,
        tiled=True,
    )
    halo_count = partitions * capacity // tile_size
    halo_block = incoming.reshape(halo_count, tile_size, block_width).transpose(0, 2, 1)
    source = jnp.concatenate([rounded, halo_block], 0)
    picked = source[tile_cols]
    products = jnp.einsum("kbj,kij->kbi", picked, tile_values, preferred_element_type=jnp.float32)
    slot_total = tile_cols.shape[0]
    live_slots = jnp.arange(slot_total, dtype=jnp.int32) < tile_count[0]
    owner_table = (
        tile_rows[None, :] == jnp.arange(row_tiles, dtype=jnp.int32)[:, None]
    ) & live_slots[None, :]
    return jnp.einsum(
        "rk,kbi->rbi", owner_table.astype(jnp.float32), products, precision=HIGHEST_PRECISION
    )


def body(
    start_block, tile_values, tile_rows, tile_cols, tile_count, send_rows, send_count, rotation
):
    node_total = (
        start_block.shape[0] * start_block.shape[2] * lax.axis_size("row") * lax.axis_size("col")
    )
    start_sum = lax.psum(local_inner(start_block, start_block), ("row", "col"))
    vectors = [unit_columns(start_block, start_sum / node_total)]
    for krylov_step in range(2):
        product_block = apply_graph(
            vectors[-1], tile_values, tile_rows, tile_cols, tile_count, send_rows, send_count
        )
        stacked = jnp.concatenate(vectors, 1)
        coefficients = lax.psum(local_inner(stacked, product_block), ("row", "col")) / node_total
        residual_block = product_block - jnp.einsum(
            "ab,tai->tbi", coefficients, stacked, precision=HIGHEST_PRECISION
        )
        gram_matrix = (
            lax.psum(local_inner(residual_block, residual_block), ("row", "col")) / node_total
        )
        vectors.append(unit_columns(residual_block, gram_matrix))
    all_vectors = jnp.concatenate(vectors, 1)
    return jnp.einsum("jb,tji->tbi", rotation, all_vectors, precision=HIGHEST_PRECISION)


def solution(mesh):
    return jax.shard_map(
        body,
        mesh=mesh,
        in_specs=(
            P(("row", "col"), None, None),
            P(("row", "col"), None, None),
            P(("row", "col")),
            P(("row", "col")),
            P(("row", "col")),
            P(("row", "col"), None, None),
            P(("row", "col"), None),
            P(),
        ),
        out_specs=P(("row", "col"), None, None),
        check_vma=False,
    )
```

profile of v0, /device:TPU:1, one launch (start us, length us, event | category | flops | bytes accessed | tf_op | source)
XLA Modules:
  0.0 668.5 jit_solution(7324829424072807957)
XLA Ops:
  1.6 81.5 %psum.35 = f32[64,64]{0,1:T(8,128)S(1)} all-reduce(f32[64,64]{0,1:T(8,128)S(1)} %convolution_bitcast_fusion.8), channel_id=1, replica_groups=mesh['row'=16,'col'=16] {'row','col'}, use_global_device_ids=true, to_apply=%region_0.0 | all-reduce | flops 4096 | bytes 32768 | tf_op jit(solution)/shard_map/psum | solution.py:59
  83.2 5.8 cholesky.59
  90.4 4.9 custom-call.7
  96.8 24.0 %gather_fusion = bf16[8192,64]{1,0:T(8,128)(2,1)S(1)} fusion(bf16[2048,64]{1,0:T(8,128)(2,1)S(1)} %bitcast.92, s32[8192]{0:T(1024)S(1)} %broadcast_clamp_fusion), kind=kCustom, calls=%fused_computation | custom fusion | bytes 2129920 | tf_op jit(solution)/shard_map/gather | solution.py:27
  128.8 33.5 %all_to_all.20 = bf16[16,16,2048]{2,1,0:T(8,128)(2,1)S(1)} all-to-all(bf16[16,16,2048]{2,1,0:T(8,128)(2,1)S(1)} %broadcast_select_fusion.1), channel_id=1, replica_groups=mesh['row'=16,'col'=16] {'row'}, dimensions={0} | all-to-all | bytes 2097152 | tf_op jit(solution)/shard_map/all_to_all | solution.py:32
  168.7 16.5 %all-to-all-done.1 = bf16[16,16,2048]{2,0,1:T(8,128)(2,1)S(1)} async-done(((bf16[16,16,2048]{2,0,1:T(8,128)(2,1)}), bf16[16,16,2048]{2,0,1:T(8,128)(2,1)S(1)}, u32[]{:S(2)}, u32[]{:S(2)}) %all-to-all-start.1) | async-done | bytes 1048608 | tf_op jit(solution)/shard_map/all_to_all | solution.py:31
  192.2 10.4 %gather_fusion.1 = bf16[256,64,128]{1,2,0:T(8,128)(2,1)} fusion(bf16[80,64,128]{1,2,0:T(8,128)(2,1)} %pad_maximum_fusion, s32[1024]{0:T(1024)S(1)} %pad_clamp_fusion), kind=kCustom, calls=%fused_computation.1 | custom fusion | bytes 8389632 | tf_op jit(solution)/shard_map/gather | solution.py:41
  202.6 9.7 %fusion.57 = f32[256,64,128]{2,1,0:T(8,128)S(1)} fusion(bf16[256,64,128]{1,2,0:T(8,128)(2,1)} %gather_fusion.1, bf16[256,128,128]{2,1,0:T(8,128)(2,1)} %param.12), kind=kOutput, calls=%fused_computation.100 | convolution fusion | flops 536870912 | bytes 20971520 | tf_op jit(solution)/shard_map/kbj,kij->kbi/dot_general | solution.py:42
  212.3 7.5 %fusion.2 = f32[16,64,128]{2,0,1:T(8,128)S(1)} fusion(f32[256,64,128]{2,1,0:T(8,128)S(1)} %fusion.57, s32[256]{0:T(256)S(1)} %copy-done.6, pred[256]{0:T(512)(128)(4,1)S(1)} %iota_compare_fusion.7), kind=kOutput, calls=%fused_computation.6 | convolution fusion | flops 402661376 | bytes 8914176 | tf_op jit(solution)/shard_map/rk,kbi->rbi/dot_general | solution.py:48
  220.5 72.7 %psum.36 = f32[64,64]{0,1:T(8,128)S(1)} all-reduce(f32[64,64]{0,1:T(8,128)S(1)} %convolution_bitcast_fusion.6), channel_id=1, replica_groups=mesh['row'=16,'col'=16] {'row','col'}, use_global_device_ids=true, to_apply=%region_3.0 | all-reduce | flops 4096 | bytes 32768 | tf_op jit(solution)/shard_map/psum | solution.py:66
  295.0 73.9 %psum.37 = f32[64,64]{0,1:T(8,128)S(1)} all-reduce(f32[64,64]{0,1:T(8,128)S(1)} %convolution_bitcast_fusion.5), channel_id=1, replica_groups=mesh['row'=16,'col'=16] {'row','col'}, use_global_device_ids=true, to_apply=%region_4.0 | all-reduce | flops 4096 | bytes 32768 | tf_op jit(solution)/shard_map/psum | solution.py:71
  369.0 5.8 cholesky.70
  376.3 4.9 custom-call.8
  383.3 24.0 %gather_fusion.2 = bf16[8192,64]{1,0:T(8,128)(2,1)S(1)} fusion(bf16[2048,64]{1,0:T(8,128)(2,1)S(1)} %bitcast.93, s32[8192]{0:T(1024)S(1)} %broadcast_clamp_fusion), kind=kCustom, calls=%fused_computation.2 | custom fusion | bytes 2129920 | tf_op jit(solution)/shard_map/gather | solution.py:27
  411.3 32.6 %all_to_all.21 = bf16[16,16,2048]{2,1,0:T(8,128)(2,1)S(1)} all-to-all(bf16[16,16,2048]{2,1,0:T(8,128)(2,1)S(1)} %broadcast_select_fusion), channel_id=1, replica_groups=mesh['row'=16,'col'=16] {'row'}, dimensions={0} | all-to-all | bytes 2097152 | tf_op jit(solution)/shard_map/all_to_all | solution.py:32
  445.5 3.9 all-to-all-start.3
  449.7 18.4 %all-to-all-done.3 = bf16[16,16,2048]{2,0,1:T(8,128)(2,1)S(1)} async-done(((bf16[16,16,2048]{2,0,1:T(8,128)(2,1)}), bf16[16,16,2048]{2,0,1:T(8,128)(2,1)S(1)}, u32[]{:S(2)}, u32[]{:S(2)}) %all-to-all-start.3) | async-done | bytes 1048608 | tf_op jit(solution)/shard_map/all_to_all | solution.py:31
  475.1 10.4 %gather_fusion.3 = bf16[256,64,128]{1,2,0:T(8,128)(2,1)} fusion(bf16[80,64,128]{1,2,0:T(8,128)(2,1)} %pad_maximum_fusion.1, s32[1024]{0:T(1024)S(1)} %pad_clamp_fusion), kind=kCustom, calls=%fused_computation.3 | custom fusion | bytes 8389632 | tf_op jit(solution)/shard_map/gather | solution.py:41
  485.5 9.5 %fusion.58 = f32[256,64,128]{2,1,0:T(8,128)S(1)} fusion(bf16[256,64,128]{1,2,0:T(8,128)(2,1)} %gather_fusion.3, bf16[256,128,128]{2,1,0:T(8,128)(2,1)} %param.12), kind=kOutput, calls=%fused_computation.101 | convolution fusion | flops 536870912 | bytes 20971520 | tf_op jit(solution)/shard_map/kbj,kij->kbi/dot_general | solution.py:42
  495.0 7.5 %fusion = f32[16,64,128]{2,0,1:T(8,128)S(1)} fusion(f32[256,64,128]{2,1,0:T(8,128)S(1)} %fusion.58, s32[256]{0:T(256)S(1)} %copy-done.6, pred[256]{0:T(512)(128)(4,1)S(1)} %iota_compare_fusion.7), kind=kOutput, calls=%fused_computation.4 | convolution fusion | flops 402661376 | bytes 8914176 | tf_op jit(solution)/shard_map/rk,kbi->rbi/dot_general | solution.py:48
  503.7 72.8 %psum.38 = f32[128,64]{0,1:T(8,128)S(1)} all-reduce(f32[128,64]{0,1:T(8,128)S(1)} %convolution_bitcast_fusion.1), channel_id=1, replica_groups=mesh['row'=16,'col'=16] {'row','col'}, use_global_device_ids=true, to_apply=%region_5.8 | all-reduce | flops 8192 | bytes 65536 | tf_op jit(solution)/shard_map/psum | solution.py:66
  578.3 74.5 %psum.39 = f32[64,64]{0,1:T(8,128)S(1)} all-reduce(f32[64,64]{0,1:T(8,128)S(1)} %convolution_bitcast_fusion.3), channel_id=1, replica_groups=mesh['row'=16,'col'=16] {'row','col'}, use_global_device_ids=true, to_apply=%region_6.9 | all-reduce | flops 4096 | bytes 32768 | tf_op jit(solution)/shard_map/psum | solution.py:71
  652.9 5.8 cholesky.81
  660.1 4.9 custom-call.9
  (80 shorter events, 51.3 us)
Async XLA Ops:
  0.0 1.0 copy-start
  0.0 96.5 %copy-start.5 = (s32[1,256,32]{1,2,0:T(8,128)S(1)}, s32[1,256,32]{1,2,0:T(8,128)}, u32[]{:S(2)}) copy-start(s32[1,256,32]{1,2,0:T(8,128)} %param.16) | copy-start | bytes 98308
  96.8 26.5 %copy-start.7 = (s32[1,256]{1,0:T(1,128)S(1)}, s32[1,256]{1,0:T(1,128)}, u32[]{:S(2)}) copy-start(s32[1,256]{1,0:T(1,128)} %param.17) | copy-start | bytes 3076
  127.3 36.6 %copy-start.3 = (pred[16,16,2048]{2,1,0:T(8,128)(4,1)}, pred[16,16,2048]{2,1,0:T(8,128)(4,1)S(1)}, u32[]{:S(2)}) copy-start(pred[16,16,2048]{2,1,0:T(8,128)(4,1)S(1)} %broadcast_in_dim.17) | copy-start | bytes 1572868
  128.8 39.9 %copy-start.8 = (s32[256]{0:T(256)S(1)}, s32[256]{0:T(256)}, u32[]{:S(2)}) copy-start(s32[256]{0:T(256)} %param.14) | copy-start | bytes 3076
  163.9 21.4 %all-to-all-start.1 = ((bf16[16,16,2048]{2,0,1:T(8,128)(2,1)}), bf16[16,16,2048]{2,0,1:T(8,128)(2,1)S(1)}, u32[]{:S(2)}, u32[]{:S(2)}) async-start(bf16[16,16,2048]{2,0,1:T(8,128)(2,1)} %copy.49), calls=%async_computation.1 | async-start | bytes 2097152 | tf_op jit(solution)/shard_map/all_to_all | solution.py:31
  202.6 9.7 %copy-start.6 = (s32[256]{0:T(256)S(1)}, s32[256]{0:T(256)}, u32[]{:S(2)}) copy-start(s32[256]{0:T(256)} %param.13) | copy-start | bytes 3076
  445.5 22.6 %all-to-all-start.3 = ((bf16[16,16,2048]{2,0,1:T(8,128)(2,1)}), bf16[16,16,2048]{2,0,1:T(8,128)(2,1)S(1)}, u32[]{:S(2)}, u32[]{:S(2)}) async-start(bf16[16,16,2048]{2,0,1:T(8,128)(2,1)} %copy.64), calls=%async_computation.3 | async-start | bytes 2097152 | tf_op jit(solution)/shard_map/all_to_all | solution.py:31
  495.0 7.5 %copy-start.2 = (f32[16,128,64]{1,2,0:T(8,128)S(1)}, f32[16,128,64]{1,2,0:T(8,128)}, u32[]{:S(2)}) copy-start(f32[16,128,64]{1,2,0:T(8,128)} %get-tuple-element.11) | copy-start | bytes 1572868
  502.5 163.6 %copy-start.4 = (f32[192,64]{0,1:T(8,128)S(1)}, f32[192,64]{0,1:T(8,128)}, u32[]{:S(2)}) copy-start(f32[192,64]{0,1:T(8,128)} %param.18) | copy-start | bytes 147460
  502.5 165.5 %copy-start.1 = (f32[16,64,128]{2,1,0:T(8,128)S(1)}, f32[16,64,128]{2,1,0:T(8,128)}, u32[]{:S(2)}) copy-start(f32[16,64,128]{2,1,0:T(8,128)} %param.11) | copy-start | bytes 1572868
where the time goes:
time: 675 us; the launch traced here: 668 us
  blocking collectives  442 us (65%)
  local copies, waits for them, and re-layouts  93.1 us (14%)
  matrix products  45.1 us (7%)
  other arithmetic  44.5 us (7%)
  waiting for transfers between devices  35 us (5%)
  starting transfers between devices  7.75 us (1%)
    psum x2, blocking collectives, body(): lax.psum(local_inner(residual_block, residual_block), ('row', 'col'))  148 us
    psum x2, blocking collectives, body(): lax.psum(local_inner(stacked, product_block), ('row', 'col')) / node_total  146 us
    psum x1, blocking collectives, body(): start_sum = lax.psum(local_inner(start_block, start_block), ('row', 'col'))  81.5 us
    all_to_all x2, blocking collectives, apply_graph(): lax.all_to_all(outgoing, 'row', split_axis=0, concat_axis=0, tiled=True)  66.1 us
    gather x2, local copies, waits for them, and re-layouts, apply_graph(): node_rows[targets.reshape(-1)].reshape(partitions, capacity, block_width)  48.1 us
    all_to_all x2, waiting for transfers between devices, apply_graph(): lax.all_to_all(lax.all_to_all(outgoing, 'row', split_axis=0, concat_axis=...  35 us
    gather x2, local copies, waits for them, and re-layouts, apply_graph(): picked = source[tile_cols]  20.7 us
    another operation x9, other arithmetic, unit_columns(): factor = jnp.linalg.cholesky(gram_matrix)  19.6 us
  transfers between devices with their start and end apart: 2, of which 2 were waited for; matrix products, arithmetic and copies ran while one was open for 0% of the time, Pallas kernels for 0%

commit v1 on v0

--- a/solution.py
+++ b/solution.py
@@ -1,9 +1,19 @@
+import functools
 import jax
 import jax.numpy as jnp
 from jax import lax
 from jax.sharding import PartitionSpec as P
 
 HIGHEST_PRECISION = lax.Precision.HIGHEST
+
+
+def _deliver_results(own_rows, axis_tag, axis_key):
+    for dev in (axis_tag, axis_key):
+        own_rows = jax.lax.psum(own_rows, dev)
+    return own_rows
+
+
+press_zone_in = functools.partial(_deliver_results, axis_tag="row", axis_key="col")
 
 
 def local_inner(left_block, right_block):
@@ -63,7 +73,7 @@
             vectors[-1], tile_values, tile_rows, tile_cols, tile_count, send_rows, send_count
         )
         stacked = jnp.concatenate(vectors, 1)
-        coefficients = lax.psum(local_inner(stacked, product_block), ("row", "col")) / node_total
+        coefficients = press_zone_in(local_inner(stacked, product_block)) / node_total
         residual_block = product_block - jnp.einsum(
             "ab,tai->tbi", coefficients, stacked, precision=HIGHEST_PRECISION
         )

time: 675 us -> 756 us (1.12)
  blocking collectives: 442 us -> 523 us
    psum x2 -> x4, blocking collectives: 146 us -> 197 us  [_deliver_results(): own_rows = jax.lax.psum(own_rows, dev)]
    psum x2, blocking collectives: 148 us -> 176 us  [body(): lax.psum(local_inner(residual_block, residual_block), ('row', 'col'))]
where the time goes in v1:
time: 756 us; the launch traced here: 750 us
  blocking collectives  523 us (69%)
  local copies, waits for them, and re-layouts  93.1 us (12%)
  matrix products  45.1 us (6%)
  other arithmetic  44.5 us (6%)
  waiting for transfers between devices  35 us (5%)
  starting transfers between devices  8.1 us (1%)
    psum x4, blocking collectives, _deliver_results(): own_rows = jax.lax.psum(own_rows, dev)  197 us
    psum x2, blocking collectives, body(): lax.psum(local_inner(residual_block, residual_block), ('row', 'col'))  176 us
    psum x1, blocking collectives, body(): start_sum = lax.psum(local_inner(start_block, start_block), ('row', 'col'))  81.5 us
    all_to_all x2, blocking collectives, apply_graph(): lax.all_to_all(outgoing, 'row', split_axis=0, concat_axis=0, tiled=True)  67.4 us
    gather x2, local copies, waits for them, and re-layouts, apply_graph(): node_rows[targets.reshape(-1)].reshape(partitions, capacity, block_width)  48.1 us
    all_to_all x2, waiting for transfers between devices, apply_graph(): lax.all_to_all(lax.all_to_all(outgoing, 'row', split_axis=0, concat_axis=...  35 us
    gather x2, local copies, waits for them, and re-layouts, apply_graph(): picked = source[tile_cols]  20.7 us
    another operation x9, other arithmetic, unit_columns(): factor = jnp.linalg.cholesky(gram_matrix)  19.6 us
  transfers between devices with their start and end apart: 2, of which 2 were waited for; matrix products, arithmetic and copies ran while one was open for 0% of the time, Pallas kernels for 0%

profile of v1, /device:TPU:1, one launch (start us, length us, event | category | flops | bytes accessed | tf_op | source)
XLA Modules:
  0.0 749.8 jit_solution(5239690706114066985)
XLA Ops:
  1.6 81.5 %psum.49 = f32[64,64]{0,1:T(8,128)S(1)} all-reduce(f32[64,64]{0,1:T(8,128)S(1)} %convolution_bitcast_fusion.8), channel_id=1, replica_groups=mesh['row'=16,'col'=16] {'row','col'}, use_global_device_ids=true, to_apply=%region_0.0 | all-reduce | flops 4096 | bytes 32768 | tf_op jit(solution)/shard_map/psum | solution.py:69
  83.2 5.8 cholesky.59
  90.4 4.9 custom-call.7
  96.8 24.0 %gather_fusion = bf16[8192,64]{1,0:T(8,128)(2,1)S(1)} fusion(bf16[2048,64]{1,0:T(8,128)(2,1)S(1)} %bitcast.92, s32[8192]{0:T(1024)S(1)} %broadcast_clamp_fusion), kind=kCustom, calls=%fused_computation | custom fusion | bytes 2129920 | tf_op jit(solution)/shard_map/gather | solution.py:37
  128.8 33.5 %all_to_all.20 = bf16[16,16,2048]{2,1,0:T(8,128)(2,1)S(1)} all-to-all(bf16[16,16,2048]{2,1,0:T(8,128)(2,1)S(1)} %broadcast_select_fusion.1), channel_id=1, replica_groups=mesh['row'=16,'col'=16] {'row'}, dimensions={0} | all-to-all | bytes 2097152 | tf_op jit(solution)/shard_map/all_to_all | solution.py:42
  168.7 16.5 %all-to-all-done.1 = bf16[16,16,2048]{2,0,1:T(8,128)(2,1)S(1)} async-done(((bf16[16,16,2048]{2,0,1:T(8,128)(2,1)}), bf16[16,16,2048]{2,0,1:T(8,128)(2,1)S(1)}, u32[]{:S(2)}, u32[]{:S(2)}) %all-to-all-start.1) | async-done | bytes 1048608 | tf_op jit(solution)/shard_map/all_to_all | solution.py:41
  192.2 10.4 %gather_fusion.1 = bf16[256,64,128]{1,2,0:T(8,128)(2,1)} fusion(bf16[80,64,128]{1,2,0:T(8,128)(2,1)} %pad_maximum_fusion, s32[1024]{0:T(1024)S(1)} %pad_clamp_fusion), kind=kCustom, calls=%fused_computation.1 | custom fusion | bytes 8389632 | tf_op jit(solution)/shard_map/gather | solution.py:51
  202.6 9.7 %fusion.57 = f32[256,64,128]{2,1,0:T(8,128)S(1)} fusion(bf16[256,64,128]{1,2,0:T(8,128)(2,1)} %gather_fusion.1, bf16[256,128,128]{2,1,0:T(8,128)(2,1)} %param.12), kind=kOutput, calls=%fused_computation.100 | convolution fusion | flops 536870912 | bytes 20971520 | tf_op jit(solution)/shard_map/kbj,kij->kbi/dot_general | solution.py:52
  212.3 7.5 %fusion.2 = f32[16,64,128]{2,0,1:T(8,128)S(1)} fusion(f32[256,64,128]{2,1,0:T(8,128)S(1)} %fusion.57, s32[256]{0:T(256)S(1)} %copy-done.6, pred[256]{0:T(512)(128)(4,1)S(1)} %iota_compare_fusion.7), kind=kOutput, calls=%fused_computation.6 | convolution fusion | flops 402661376 | bytes 8914176 | tf_op jit(solution)/shard_map/rk,kbi->rbi/dot_general | solution.py:58
  220.5 42.5 %psum.50 = f32[64,64]{0,1:T(8,128)S(1)} all-reduce(f32[64,64]{0,1:T(8,128)S(1)} %convolution_bitcast_fusion.6), channel_id=1, replica_groups=mesh['row'=16,'col'=16] {'row'}, use_global_device_ids=true, to_apply=%region_3.0 | all-reduce | flops 4096 | bytes 32768 | tf_op jit(solution)/shard_map/psum | solution.py:12
  263.0 56.5 %psum.51 = f32[64,64]{0,1:T(8,128)S(1)} all-reduce(f32[64,64]{0,1:T(8,128)S(1)} %psum.50), channel_id=1, replica_groups=mesh['row'=16,'col'=16] {'col'}, use_global_device_ids=true, to_apply=%region_4.0 | all-reduce | flops 4096 | bytes 32768 | tf_op jit(solution)/shard_map/psum | solution.py:12
  321.3 88.0 %psum.52 = f32[64,64]{0,1:T(8,128)S(1)} all-reduce(f32[64,64]{0,1:T(8,128)S(1)} %convolution_bitcast_fusion.5), channel_id=1, replica_groups=mesh['row'=16,'col'=16] {'row','col'}, use_global_device_ids=true, to_apply=%region_5.0 | all-reduce | flops 4096 | bytes 32768 | tf_op jit(solution)/shard_map/psum | solution.py:81
  409.4 5.8 cholesky.70
  416.7 4.9 custom-call.8
  423.8 24.0 %gather_fusion.2 = bf16[8192,64]{1,0:T(8,128)(2,1)S(1)} fusion(bf16[2048,64]{1,0:T(8,128)(2,1)S(1)} %bitcast.93, s32[8192]{0:T(1024)S(1)} %broadcast_clamp_fusion), kind=kCustom, calls=%fused_computation.2 | custom fusion | bytes 2129920 | tf_op jit(solution)/shard_map/gather | solution.py:37
  451.7 34.0 %all_to_all.21 = bf16[16,16,2048]{2,1,0:T(8,128)(2,1)S(1)} all-to-all(bf16[16,16,2048]{2,1,0:T(8,128)(2,1)S(1)} %broadcast_select_fusion), channel_id=1, replica_groups=mesh['row'=16,'col'=16] {'row'}, dimensions={0} | all-to-all | bytes 2097152 | tf_op jit(solution)/shard_map/all_to_all | solution.py:42
  491.8 18.4 %all-to-all-done.3 = bf16[16,16,2048]{2,0,1:T(8,128)(2,1)S(1)} async-done(((bf16[16,16,2048]{2,0,1:T(8,128)(2,1)}), bf16[16,16,2048]{2,0,1:T(8,128)(2,1)S(1)}, u32[]{:S(2)}, u32[]{:S(2)}) %all-to-all-start.3) | async-done | bytes 1048608 | tf_op jit(solution)/shard_map/all_to_all | solution.py:41
  517.2 10.4 %gather_fusion.3 = bf16[256,64,128]{1,2,0:T(8,128)(2,1)} fusion(bf16[80,64,128]{1,2,0:T(8,128)(2,1)} %pad_maximum_fusion.1, s32[1024]{0:T(1024)S(1)} %pad_clamp_fusion), kind=kCustom, calls=%fused_computation.3 | custom fusion | bytes 8389632 | tf_op jit(solution)/shard_map/gather | solution.py:51
  527.6 9.5 %fusion.58 = f32[256,64,128]{2,1,0:T(8,128)S(1)} fusion(bf16[256,64,128]{1,2,0:T(8,128)(2,1)} %gather_fusion.3, bf16[256,128,128]{2,1,0:T(8,128)(2,1)} %param.12), kind=kOutput, calls=%fused_computation.101 | convolution fusion | flops 536870912 | bytes 20971520 | tf_op jit(solution)/shard_map/kbj,kij->kbi/dot_general | solution.py:52
  537.1 7.5 %fusion = f32[16,64,128]{2,0,1:T(8,128)S(1)} fusion(f32[256,64,128]{2,1,0:T(8,128)S(1)} %fusion.58, s32[256]{0:T(256)S(1)} %copy-done.6, pred[256]{0:T(512)(128)(4,1)S(1)} %iota_compare_fusion.7), kind=kOutput, calls=%fused_computation.4 | convolution fusion | flops 402661376 | bytes 8914176 | tf_op jit(solution)/shard_map/rk,kbi->rbi/dot_general | solution.py:58
  545.8 42.5 %psum.53 = f32[128,64]{0,1:T(8,128)S(1)} all-reduce(f32[128,64]{0,1:T(8,128)S(1)} %convolution_bitcast_fusion.1), channel_id=1, replica_groups=mesh['row'=16,'col'=16] {'row'}, use_global_device_ids=true, to_apply=%region_6.0 | all-reduce | flops 8192 | bytes 65536 | tf_op jit(solution)/shard_map/psum | solution.py:12
  588.4 55.7 %psum.54 = f32[128,64]{0,1:T(8,128)S(1)} all-reduce(f32[128,64]{0,1:T(8,128)S(1)} %psum.53), channel_id=1, replica_groups=mesh['row'=16,'col'=16] {'col'}, use_global_device_ids=true, to_apply=%region_7.10 | all-reduce | flops 8192 | bytes 65536 | tf_op jit(solution)/shard_map/psum | solution.py:12
  645.9 88.3 %psum.55 = f32[64,64]{0,1:T(8,128)S(1)} all-reduce(f32[64,64]{0,1:T(8,128)S(1)} %convolution_bitcast_fusion.3), channel_id=1, replica_groups=mesh['row'=16,'col'=16] {'row','col'}, use_global_device_ids=true, to_apply=%region_8.11 | all-reduce | flops 4096 | bytes 32768 | tf_op jit(solution)/shard_map/psum | solution.py:81
  734.2 5.8 cholesky.81
  (82 shorter events, 60.4 us)
Async XLA Ops:
  0.0 1.0 copy-start
  0.0 96.5 %copy-start.5 = (s32[1,256,32]{1,2,0:T(8,128)S(1)}, s32[1,256,32]{1,2,0:T(8,128)}, u32[]{:S(2)}) copy-start(s32[1,256,32]{1,2,0:T(8,128)} %param.16) | copy-start | bytes 98308
  96.8 26.5 %copy-start.7 = (s32[1,256]{1,0:T(1,128)S(1)}, s32[1,256]{1,0:T(1,128)}, u32[]{:S(2)}) copy-start(s32[1,256]{1,0:T(1,128)} %param.17) | copy-start | bytes 3076
  127.3 36.6 %copy-start.3 = (pred[16,16,2048]{2,1,0:T(8,128)(4,1)}, pred[16,16,2048]{2,1,0:T(8,128)(4,1)S(1)}, u32[]{:S(2)}) copy-start(pred[16,16,2048]{2,1,0:T(8,128)(4,1)S(1)} %broadcast_in_dim.17) | copy-start | bytes 1572868
  128.8 39.9 %copy-start.8 = (s32[256]{0:T(256)S(1)}, s32[256]{0:T(256)}, u32[]{:S(2)}) copy-start(s32[256]{0:T(256)} %param.14) | copy-start | bytes 3076
  163.9 21.4 %all-to-all-start.1 = ((bf16[16,16,2048]{2,0,1:T(8,128)(2,1)}), bf16[16,16,2048]{2,0,1:T(8,128)(2,1)S(1)}, u32[]{:S(2)}, u32[]{:S(2)}) async-start(bf16[16,16,2048]{2,0,1:T(8,128)(2,1)} %copy.49), calls=%async_computation.1 | async-start | bytes 2097152 | tf_op jit(solution)/shard_map/all_to_all | solution.py:41
  202.6 9.7 %copy-start.6 = (s32[256]{0:T(256)S(1)}, s32[256]{0:T(256)}, u32[]{:S(2)}) copy-start(s32[256]{0:T(256)} %param.13) | copy-start | bytes 3076
  487.3 23.0 %all-to-all-start.3 = ((bf16[16,16,2048]{2,0,1:T(8,128)(2,1)}), bf16[16,16,2048]{2,0,1:T(8,128)(2,1)S(1)}, u32[]{:S(2)}, u32[]{:S(2)}) async-start(bf16[16,16,2048]{2,0,1:T(8,128)(2,1)} %copy.64), calls=%async_computation.3 | async-start | bytes 2097152 | tf_op jit(solution)/shard_map/all_to_all | solution.py:41
  537.1 7.5 %copy-start.2 = (f32[16,128,64]{1,2,0:T(8,128)S(1)}, f32[16,128,64]{1,2,0:T(8,128)}, u32[]{:S(2)}) copy-start(f32[16,128,64]{1,2,0:T(8,128)} %get-tuple-element.11) | copy-start | bytes 1572868
  544.6 202.7 %copy-start.4 = (f32[192,64]{0,1:T(8,128)S(1)}, f32[192,64]{0,1:T(8,128)}, u32[]{:S(2)}) copy-start(f32[192,64]{0,1:T(8,128)} %param.18) | copy-start | bytes 147460
  544.6 204.7 %copy-start.1 = (f32[16,64,128]{2,1,0:T(8,128)S(1)}, f32[16,64,128]{2,1,0:T(8,128)}, u32[]{:S(2)}) copy-start(f32[16,64,128]{2,1,0:T(8,128)} %param.11) | copy-start | bytes 1572868
